TPU v7x, 32 devices: a whole 2x2x4 slice. The times are simulated.
32 devices in a mesh: blk: 4 (over y, x), strata: 8 (over z, core).
Axes of the slice: x: 2, y: 2, z: 4, core: 2. Of those that a mesh axis runs over, the one named last changes fastest.
Arguments:
- user_factors: bfloat16 [4096, 256], P('blk'), may hold values from -1.5 to 1.5
- item_factors: bfloat16 [8192, 256], P(('blk', 'strata')), may hold values from -1.5 to 1.5
- ratings: bfloat16 [4, 4, 8, 8, 128, 128], P('blk', None, 'strata'), may hold values from -6 to 6
- tile_user: int32 [4, 4, 8, 8], P('blk', None, 'strata'), may hold values from 0 to 7
- tile_item: int32 [4, 4, 8, 8], P('blk', None, 'strata'), may hold values from 0 to 1
- tile_count: int32 [4, 4, 8], P('blk', None, 'strata'), may hold values from 1 to 8, 40 in all within a row
Outputs:
- user_grad: float32 [4096, 256], P('blk')
- item_grad: float32 [8192, 256], P(('blk', 'strata'))
Inputs may be any that keep to these rules, and one draw needn't show every extreme that they name: `tile_count`: for each user block and panel index, the counts over the strata are uneven and one of them equals 8.
All inputs are finite; a program needn't handle non-finite values.
Results may differ from a plain program's by a relative error of at most 0.0012.
Values may be sent and summed in bfloat16 or wider, within the bound.
A program may use at most 64 MiB of HBM per device.

v0:
```python
import jax
import jax.numpy as jnp
from jax import lax
from jax.sharding import PartitionSpec as P


def tile_terms(user_tiles, panel_tiles, rating_tiles, rows, cols, count):
    slots = rating_tiles.shape[0]
    tile = rating_tiles.shape[-1]
    picked_users = jnp.take(user_tiles, rows, axis=0)
    picked_items = jnp.take(panel_tiles, cols, axis=0)
    predicted = jnp.einsum(
        "kar,kbr->kab", picked_users, picked_items, preferred_element_type=jnp.float32
    )
    live = (jnp.arange(slots) < count).astype(jnp.float32)
    residue = ((predicted - rating_tiles.astype(jnp.float32)) * live[:, None, None]).astype(
        jnp.bfloat16
    )
    user_part = (
        jnp.einsum("kab,kbr->kar", residue, picked_items, preferred_element_type=jnp.float32) / tile
    )
    item_part = (
        jnp.einsum("kab,kar->kbr", residue, picked_users, preferred_element_type=jnp.float32) / tile
    )
    user_hot = (rows[:, None] == jnp.arange(user_tiles.shape[0])[None, :]).astype(jnp.float32)
    item_hot = (cols[:, None] == jnp.arange(panel_tiles.shape[0])[None, :]).astype(jnp.float32)
    user_sum = jnp.einsum("ku,kar->uar", user_hot, user_part, precision=lax.Precision.HIGHEST)
    item_sum = jnp.einsum("kp,kbr->pbr", item_hot, item_part, precision=lax.Precision.HIGHEST)
    return (user_sum, item_sum)


def settle_early(user_total, early):
    return (user_total, early)


def body(user_factors, item_factors, ratings, tile_user, tile_item, tile_count):
    steps = lax.axis_size("blk")
    tile = ratings.shape[-1]
    rank = user_factors.shape[1]
    panel_rows = item_factors.shape[0]
    user_tiles = user_factors.reshape(-1, tile, rank)
    rating_sets = ratings[0, :, 0]
    row_sets = tile_user[0, :, 0]
    col_sets = tile_item[0, :, 0]
    count_sets = tile_count[0, :, 0]
    user_total = jnp.zeros(user_tiles.shape, jnp.float32)
    early = None
    gathered = lax.all_gather(item_factors, "blk", axis=0, tiled=True)
    pieces = []
    for source in range(steps):
        panel = gathered[source * panel_rows : (source + 1) * panel_rows]
        rating_tiles = lax.dynamic_index_in_dim(rating_sets, source, 0, keepdims=False)
        rows = lax.dynamic_index_in_dim(row_sets, source, 0, keepdims=False)
        cols = lax.dynamic_index_in_dim(col_sets, source, 0, keepdims=False)
        count = lax.dynamic_index_in_dim(count_sets, source, 0, keepdims=False)
        user_part, item_part = tile_terms(
            user_tiles, panel.reshape(-1, tile, rank), rating_tiles, rows, cols, count
        )
        user_total = user_total + user_part
        pieces.append(item_part.reshape(panel_rows, rank))
        user_total, early = settle_early(user_total, early)
    item_grad = lax.psum_scatter(
        jnp.concatenate(pieces, axis=0), "blk", scatter_dimension=0, tiled=True
    )
    user_grad = lax.psum(user_total, "strata")
    return (user_grad.reshape(-1, rank), item_grad)


def solution(mesh):
    in_specs = (
        P("blk", None),
        P(("blk", "strata"), None),
        P("blk", None, "strata", None, None, None),
        P("blk", None, "strata", None),
        P("blk", None, "strata", None),
        P("blk", None, "strata"),
    )
    out_specs = (P("blk", None), P(("blk", "strata"), None))
    return jax.shard_map(body, mesh=mesh, in_specs=in_specs, out_specs=out_specs, check_vma=False)
```

profile of v0, /device:TPU:0, one launch (start us, length us, event | category | flops | bytes accessed | tf_op | source)
XLA Modules:
  0.0 119.4 jit_solution(5555860137044684791)
XLA Ops:
  9.5 11.8 %all_gather.3 = bf16[1024,256]{1,0:T(8,128)(2,1)S(1)} all-gather(bf16[256,256]{1,0:T(8,128)(2,1)} %param.11), channel_id=1, replica_groups=mesh['blk'=4,'strata'=8] {'blk'}, dimensions={0}, use_global_device_ids=true | all-gather | bytes 655360 | tf_op jit(solution)/shard_map/all_gather | solution.py:48
  23.3 1.4 %gather_fusion.4 = bf16[8,128,256]{2,1,0:T(8,128)(2,1)} fusion(bf16[8,128,256]{2,1,0:T(8,128)(2,1)S(1)} %bitcast.100, s32[1024]{0:T(1024)S(1)} %get-tuple-element.49), kind=kCustom, calls=%fused_computation.3.clone | custom fusion | bytes 1048608 | tf_op jit(solution)/shard_map/jit(_take)/gather | solution.py:10
  28.5 1.4 %gather_fusion.1 = bf16[8,128,256]{2,1,0:T(8,128)(2,1)} fusion(bf16[2,128,256]{2,1,0:T(8,128)(2,1)S(1)} %bitcast.106, s32[1024]{0:T(1024)S(1)} %get-tuple-element.55), kind=kCustom, calls=%fused_computation.1.clone | custom fusion | bytes 1048608 | tf_op jit(solution)/shard_map/jit(_take)/gather | solution.py:11
  29.9 1.5 %fusion.4 = bf16[8,128,128]{2,1,0:T(8,128)(2,1)S(1)} fusion(f32[8]{0:T(128)S(1)} %compare_convert_fusion.3, bf16[1,4,1,8,128,128]{5,4,3,2,1,0:T(8,128)(2,1)} %param.12, bf16[8,128,256]{2,1,0:T(8,128)(2,1)S(1)} %gather_fusion, pred[8]{0:T(512)(128)(4,1)S(1)} %get-tuple-element.42, bf16[8,128,256]{2,1,0:T(8,128)(2,1)} %gather_fusion.1, ...), kind=kOutput, calls=%fused_computation.19 | convolution fusion | flops 68157440 | bytes 1572912 | tf_op jit(solution)/shard_map/kar,kbr->kab/dot_general | solution.py:12
  31.4 1.5 %fusion.22 = f32[8,128,256]{2,1,0:T(8,128)S(1)} fusion(bf16[8,128,128]{2,1,0:T(8,128)(2,1)S(1)} %fusion.4, bf16[8,128,256]{2,1,0:T(8,128)(2,1)} %gather_fusion.1, pred[8]{0:T(512)(128)(4,1)S(1)} %get-tuple-element.36), kind=kOutput, calls=%fused_computation.54 | convolution fusion | flops 67371008 | bytes 1835016 | tf_op jit(solution)/shard_map/kab,kbr->kar/dot_general | solution.py:20
  32.9 1.4 %gather_fusion.3 = bf16[8,128,256]{2,1,0:T(8,128)(2,1)} fusion(bf16[2,128,256]{2,1,0:T(8,128)(2,1)S(1)} %bitcast.105, s32[1024]{0:T(1024)S(1)} %get-tuple-element.54), kind=kCustom, calls=%fused_computation.5.clone | custom fusion | bytes 1048608 | tf_op jit(solution)/shard_map/jit(_take)/gather | solution.py:11
  34.3 1.6 %fusion.5 = bf16[8,128,128]{2,1,0:T(8,128)(2,1)S(1)} fusion(f32[8]{0:T(128)S(1)} %compare_convert_fusion.2, bf16[1,4,1,8,128,128]{5,4,3,2,1,0:T(8,128)(2,1)} %param.12, bf16[8,128,256]{2,1,0:T(8,128)(2,1)S(1)} %gather_fusion.2, pred[8]{0:T(512)(128)(4,1)S(1)} %get-tuple-element.40, bf16[8,128,256]{2,1,0:T(8,128)(2,1)} %gather_fusion.3, ...), kind=kOutput, calls=%fused_computation.20 | convolution fusion | flops 68157440 | bytes 1572912 | tf_op jit(solution)/shard_map/kar,kbr->kab/dot_general | solution.py:12
  36.5 1.4 %gather_fusion.5 = bf16[8,128,256]{2,1,0:T(8,128)(2,1)} fusion(bf16[2,128,256]{2,1,0:T(8,128)(2,1)S(1)} %bitcast.104, s32[1024]{0:T(1024)S(1)} %get-tuple-element.53), kind=kCustom, calls=%fused_computation.6.clone | custom fusion | bytes 1048608 | tf_op jit(solution)/shard_map/jit(_take)/gather | solution.py:11
  37.9 1.7 %fusion.6 = bf16[8,128,128]{2,1,0:T(8,128)(2,1)S(1)} fusion(f32[8]{0:T(128)S(1)} %compare_convert_fusion.1, bf16[1,4,1,8,128,128]{5,4,3,2,1,0:T(8,128)(2,1)} %param.12, bf16[8,128,256]{2,1,0:T(8,128)(2,1)} %gather_fusion.4, pred[8]{0:T(512)(128)(4,1)S(1)} %get-tuple-element.38, bf16[8,128,256]{2,1,0:T(8,128)(2,1)} %gather_fusion.5, ...), kind=kOutput, calls=%fused_computation.21 | convolution fusion | flops 68157440 | bytes 1572912 | tf_op jit(solution)/shard_map/kar,kbr->kab/dot_general | solution.py:12
  39.7 1.3 %fusion.26 = f32[8,128,256]{2,1,0:T(8,128)} fusion(bf16[8,128,128]{2,1,0:T(8,128)(2,1)S(1)} %fusion.6, bf16[8,128,256]{2,1,0:T(8,128)(2,1)S(1)} %copy-done.9, pred[8]{0:T(512)(128)(4,1)S(1)} %get-tuple-element.32), kind=kOutput, calls=%fused_computation.58 | convolution fusion | flops 67371008 | bytes 1835016 | tf_op jit(solution)/shard_map/kab,kbr->kar/dot_general | solution.py:20
  41.0 1.4 %gather_fusion.7 = bf16[8,128,256]{2,1,0:T(8,128)(2,1)} fusion(bf16[2,128,256]{2,1,0:T(8,128)(2,1)S(1)} %bitcast.103, s32[1024]{0:T(1024)S(1)} %get-tuple-element.52), kind=kCustom, calls=%fused_computation.7.clone | custom fusion | bytes 1048608 | tf_op jit(solution)/shard_map/jit(_take)/gather | solution.py:11
  42.4 1.5 %fusion.7 = bf16[8,128,128]{2,1,0:T(8,128)(2,1)S(1)} fusion(f32[8]{0:T(128)S(1)} %compare_convert_fusion, bf16[1,4,1,8,128,128]{5,4,3,2,1,0:T(8,128)(2,1)} %param.12, bf16[8,128,256]{2,1,0:T(8,128)(2,1)S(1)} %gather_fusion.6, pred[8]{0:T(512)(128)(4,1)S(1)} %get-tuple-element.6, bf16[8,128,256]{2,1,0:T(8,128)(2,1)} %gather_fusion.7, ...), kind=kOutput, calls=%fused_computation.22 | convolution fusion | flops 68157440 | bytes 1572912 | tf_op jit(solution)/shard_map/kar,kbr->kab/dot_general | solution.py:12
  44.3 1.2 fusion.12
  45.5 1.2 convolution_add_fusion.2
  46.7 1.2 convolution_add_fusion.1
  47.9 1.2 convolution_add_fusion
  49.1 1.3 %copy.8 = f32[8,128,256]{2,1,0:T(8,128)} copy(f32[8,128,256]{2,0,1:T(8,128)S(1)} %convolution_add_fusion) | data formatting | bytes 2097152 | tf_op jit(solution)/shard_map/add | solution.py:59
  54.4 1.2 fusion.9
  55.6 1.2 fusion.8
  56.8 1.2 fusion.10
  58.1 1.2 fusion.11
  59.3 1.0 pad_maximum_fusion
  60.3 49.4 %all-reduce.2.cloned.1.call-done = f32[1024,256]{1,0:T(8,128)} async-done(((f32[1024,256]{1,0:T(8,128)}), f32[1024,256]{1,0:T(8,128)}) %all-reduce.2.cloned.1.call-update) | async-done | bytes 1048592 | tf_op jit(solution)/shard_map/psum | solution.py:65
  109.7 2.3 %copy.38 = f32[1024,256]{1,0:T(8,128)} copy(f32[1024,256]{1,0:T(8,128)} %all-reduce.2.cloned.1.call-done) | data formatting | bytes 2097152
  (70 shorter events, 12.3 us)
Async XLA Ops:
  8.0 15.3 %copy-start = (bf16[1024,256]{1,0:T(8,128)(2,1)S(1)}, bf16[1024,256]{1,0:T(8,128)(2,1)}, u32[]{:S(2)}) copy-start(bf16[1024,256]{1,0:T(8,128)(2,1)} %param.10) | copy-start | bytes 1572868
  8.0 0.8 copy-start.16
  8.0 101.7 %all-reduce.2.cloned.1.call-start = ((), (), s32[]{:S(2)}) async-start(), calls=%async_computation.1 | async-start | bytes 2097152 | tf_op jit(solution)/shard_map/psum | solution.py:65
  8.8 0.7 copy-start.17
  21.4 0.7 copy-start.18
  26.5 7.7 %copy-start.2 = (bf16[8,128,256]{2,1,0:T(8,128)(2,1)}, bf16[8,128,256]{2,1,0:T(8,128)(2,1)S(1)}, u32[]{:S(2)}) copy-start(bf16[8,128,256]{2,1,0:T(8,128)(2,1)S(1)} %gather_fusion.2) | copy-start | bytes 1572868
  27.8 2.0 %copy-start.5 = (bf16[8,128,256]{2,1,0:T(8,128)(2,1)}, bf16[8,128,256]{2,1,0:T(8,128)(2,1)S(1)}, u32[]{:S(2)}) copy-start(bf16[8,128,256]{2,1,0:T(8,128)(2,1)S(1)} %gather_fusion) | copy-start | bytes 1572868
  31.4 1.5 %copy-start.10 = (bf16[8,128,128]{2,1,0:T(8,128)(2,1)}, bf16[8,128,128]{2,1,0:T(8,128)(2,1)S(1)}, u32[]{:S(2)}) copy-start(bf16[8,128,128]{2,1,0:T(8,128)(2,1)S(1)} %fusion.4) | copy-start | bytes 786436
  34.3 1.6 %copy-start.8 = (bf16[8,128,256]{2,1,0:T(8,128)(2,1)S(1)}, bf16[8,128,256]{2,1,0:T(8,128)(2,1)}, u32[]{:S(2)}) copy-start(bf16[8,128,256]{2,1,0:T(8,128)(2,1)} %gather_fusion.3) | copy-start | bytes 1572868
  35.8 0.7 copy-start.12
  37.9 1.7 %copy-start.9 = (bf16[8,128,256]{2,1,0:T(8,128)(2,1)S(1)}, bf16[8,128,256]{2,1,0:T(8,128)(2,1)}, u32[]{:S(2)}) copy-start(bf16[8,128,256]{2,1,0:T(8,128)(2,1)} %gather_fusion.5) | copy-start | bytes 1572868
  39.6 1.4 %copy-start.14 = (bf16[8,128,128]{2,1,0:T(8,128)(2,1)}, bf16[8,128,128]{2,1,0:T(8,128)(2,1)S(1)}, u32[]{:S(2)}) copy-start(bf16[8,128,128]{2,1,0:T(8,128)(2,1)S(1)} %fusion.6) | copy-start | bytes 786436
  42.4 1.6 %copy-start.7 = (bf16[8,128,256]{2,1,0:T(8,128)(2,1)S(1)}, bf16[8,128,256]{2,1,0:T(8,128)(2,1)}, u32[]{:S(2)}) copy-start(bf16[8,128,256]{2,1,0:T(8,128)(2,1)} %gather_fusion.7) | copy-start | bytes 1572868
  45.5 1.2 %copy-start.1 = (f32[8,128,256]{2,1,0:T(8,128)S(1)}, f32[8,128,256]{2,1,0:T(8,128)}, u32[]{:S(2)}) copy-start(f32[8,128,256]{2,1,0:T(8,128)} %fusion.26) | copy-start | bytes 3145732
  50.4 1.0 copy-start.4
  50.4 1.1 copy-start.15
  50.4 59.3 %reduce-scatter.2.cloned.1.call-start = ((), (), s32[]{:S(2)}) async-start(), calls=%async_computation.2 | async-start | bytes 1310720 | tf_op jit(solution)/shard_map/reduce_scatter | solution.py:62
  51.9 1.0 copy-start.3
  51.9 1.1 copy-start.13
  53.0 1.0 copy-start.6
  53.0 1.1 copy-start.11
Sparse Core Ops, SparseCore 0:
  50.5 59.1 all-reduce.1
Sparse Core Ops, SparseCore 1:
  60.4 27.9 reduce-scatter.1
where the time goes:
time: 120 us; the launch traced here: 119 us
  waiting for transfers between devices  49.4 us (41%)
  matrix products  20.7 us (17%)
  local copies, waits for them, and re-layouts  16.9 us (14%)
  between operations  15.9 us (13%)
  blocking collectives  11.8 us (10%)
  other arithmetic  4.39 us (4%)
    psum x1, waiting for transfers between devices, body(): user_grad = lax.psum(user_total, 'strata')  49.4 us
    all_gather x1, blocking collectives, body(): gathered = lax.all_gather(item_factors, 'blk', axis=0, tiled=True)  11.8 us
    dot_general x4, matrix products, tile_terms(): jnp.einsum('kar,kbr->kab', picked_users, picked_items, preferred_element_...  6.31 us
    unnamed x39, local copies, waits for them, and re-layouts  6.27 us
    gather x4, local copies, waits for them, and re-layouts, tile_terms(): picked_items = jnp.take(panel_tiles, cols, axis=0)  5.5 us
    dot_general x4, matrix products, tile_terms(): jnp.einsum('ku,kar->uar', user_hot, user_part, precision=lax.Precision.HI...  4.7 us
    dot_general x4, matrix products, tile_terms(): jnp.einsum('kp,kbr->pbr', item_hot, item_part, precision=lax.Precision.HI...  4.68 us
    dot_general x4, matrix products, tile_terms(): jnp.einsum('kab,kbr->kar', residue, picked_items, preferred_element_type=...  3.57 us
  transfers between devices with their start and end apart: 2, of which 1 were waited for; matrix products, arithmetic and copies ran while one was open for 6% of the time, Pallas kernels for 0%

commit v1 on v0

v1 whole, which is shorter than its diff:
```python
import functools

import jax
import jax.numpy as jnp
from jax import lax
from jax.experimental import pallas as pl
from jax.experimental.pallas import tpu as pltpu
from jax.sharding import PartitionSpec as P

MESH = pl.DeviceIdType.MESH
F32 = jnp.float32
BF16 = jnp.bfloat16
CHUNK = 64
LAG = 2


def flip(place, step, size):
    other, bit = 0, 1
    while bit < size:
        other = other + bit * ((place // bit + step // bit) % 2)
        bit *= 2
    return other


def kernel(
    n_blk,
    n_strata,
    users_hbm,
    items_hbm,
    ratings_hbm,
    rows_ref,
    cols_ref,
    count_ref,
    user_out,
    item_out,
    users,
    user_table,
    panels,
    panel,
    ratings,
    predicted,
    picked_items,
    picked_users,
    by_user,
    by_item,
    user_sum,
    item_send,
    item_recv,
    pair_recv,
    side_recv,
    side_send,
    load_sem,
    rating_sem,
    gather_send,
    gather_recv,
    item_send_sem,
    item_recv_sem,
    pair_send_sem,
    pair_recv_sem,
    side_send_sem,
    side_recv_sem,
    share_send_sem,
    share_recv_sem,
):
    tile = ratings.shape[-1]
    slots = ratings.shape[1]
    user_tiles = user_table.shape[0]
    panel_tiles = panel.shape[0]
    chunks = pair_recv.shape[0] // CHUNK
    per_tile = tile // CHUNK
    blk = lax.axis_index("blk")
    strata = lax.axis_index("strata")
    core = strata % 2
    sibling = strata + 1 - 2 * core
    chip = strata // 2
    chips = n_strata // 2
    half = chips // 2
    upper = chip // half
    sign = 1 - 2 * upper
    far = (chip + sign) * 2 + core
    near = (chip - sign) * 2 + core
    depth = chip + upper * (chips - 1 - 2 * chip)
    has_near = depth > 0
    crossing = depth // (half - 1) if half > 1 else depth + 1

    load = pltpu.make_async_copy(users_hbm, users, load_sem.at[0])
    load.start()
    load_panel = pltpu.make_async_copy(items_hbm, panels.at[0], load_sem.at[1])
    load_panel.start()

    def rating_copy(step):
        source = flip(blk, step, n_blk)
        return pltpu.make_async_copy(
            ratings_hbm.at[0, source, 0], ratings.at[step], rating_sem.at[step]
        )

    def start_rating(step, carry):
        rating_copy(step).start()
        return carry

    lax.fori_loop(0, n_blk, start_rating, 0)

    barrier = pltpu.get_barrier_semaphore()

    def greet(step, carry):
        pl.semaphore_signal(
            barrier, 1, device_id=(flip(blk, step, n_blk), strata), device_id_type=MESH
        )
        return carry

    lax.fori_loop(1, n_blk, greet, 0)
    pl.semaphore_signal(barrier, 1, device_id=(blk, sibling), device_id_type=MESH)
    pl.semaphore_signal(barrier, 1, device_id=(blk, far), device_id_type=MESH)

    @pl.when(has_near)
    def _():
        pl.semaphore_signal(barrier, 1, device_id=(blk, near), device_id_type=MESH)
        pl.semaphore_wait(barrier, n_blk + 2)

    @pl.when(depth == 0)
    def _():
        pl.semaphore_wait(barrier, n_blk + 1)

    def gather_copy(step):
        return pltpu.make_async_remote_copy(
            src_ref=items_hbm,
            dst_ref=panels.at[step],
            send_sem=gather_send.at[step],
            recv_sem=gather_recv.at[step],
            device_id=(flip(blk, step, n_blk), strata),
            device_id_type=MESH,
        )

    def item_copy(step):
        return pltpu.make_async_remote_copy(
            src_ref=item_send.at[step],
            dst_ref=item_recv.at[step],
            send_sem=item_send_sem.at[step],
            recv_sem=item_recv_sem.at[step],
            device_id=(flip(blk, step, n_blk), strata),
            device_id_type=MESH,
        )

    def pair_copy(q):
        return pltpu.make_async_remote_copy(
            src_ref=user_sum.at[pl.ds((2 * q + 1 - core) * tile, tile)],
            dst_ref=pair_recv.at[pl.ds(q * tile, tile)],
            send_sem=pair_send_sem.at[q],
            recv_sem=pair_recv_sem.at[q],
            device_id=(blk, sibling),
            device_id_type=MESH,
        )

    def far_copy(c):
        return pltpu.make_async_remote_copy(
            src_ref=side_send.at[0, c],
            dst_ref=side_recv.at[crossing, c],
            send_sem=side_send_sem.at[0, c],
            recv_sem=side_recv_sem.at[crossing, c],
            device_id=(blk, far),
            device_id_type=MESH,
        )

    def near_copy(c):
        return pltpu.make_async_remote_copy(
            src_ref=side_send.at[1, c],
            dst_ref=side_recv.at[1, c],
            send_sem=side_send_sem.at[1, c],
            recv_sem=side_recv_sem.at[1, c],
            device_id=(blk, near),
            device_id_type=MESH,
        )

    def arrived(side, c):
        return pltpu.make_async_remote_copy(
            src_ref=side_send.at[0, c],
            dst_ref=side_recv.at[side, c],
            send_sem=side_send_sem.at[0, c],
            recv_sem=side_recv_sem.at[side, c],
            device_id=(blk, far),
            device_id_type=MESH,
        )

    def own_rows(c, owner):
        return pl.ds((2 * (c // per_tile) + owner) * tile + (c % per_tile) * CHUNK, CHUNK)

    def share_copy(c):
        return pltpu.make_async_remote_copy(
            src_ref=user_out.at[own_rows(c, core)],
            dst_ref=user_out.at[own_rows(c, core)],
            send_sem=share_send_sem.at[c],
            recv_sem=share_recv_sem.at[c],
            device_id=(blk, sibling),
            device_id_type=MESH,
        )

    def share_arrival(c):
        return pltpu.make_async_remote_copy(
            src_ref=user_out.at[own_rows(c, core)],
            dst_ref=user_out.at[own_rows(c, 1 - core)],
            send_sem=share_send_sem.at[c],
            recv_sem=share_recv_sem.at[c],
            device_id=(blk, sibling),
            device_id_type=MESH,
        )

    def start_gather(step, carry):
        gather_copy(step).start()
        return carry

    lax.fori_loop(1, n_blk, start_gather, 0)
    user_sum[...] = jnp.zeros_like(user_sum)

    @pl.when(depth == 0)
    def _():
        side_recv[0] = jnp.zeros(side_recv.shape[1:], F32)

    load.wait()
    load_panel.wait()

    user_table[...] = users[...].reshape(user_table.shape)

    def hot(index, place):
        same = (index == place).astype(F32)
        return jnp.full((tile, tile), same, F32).astype(BF16)

    def visit(step, carry):
        source = flip(blk, step, n_blk)

        @pl.when(step > 0)
        def _():
            gather_copy(step).wait_recv()

        rating_copy(step).wait()
        panel[...] = panels[step].reshape(panel.shape)
        for u in range(user_tiles):
            product = lax.dot_general(
                users[u * tile : (u + 1) * tile],
                panels[step],
                (((1,), (1,)), ((), ())),
                preferred_element_type=F32,
            )
            for p in range(panel_tiles):
                predicted[u * panel_tiles + p] = product[:, p * tile : (p + 1) * tile]
        for k in range(slots):
            row = rows_ref[0, source, 0, k]
            col = cols_ref[0, source, 0, k]
            live = (k < count_ref[0, source, 0]).astype(F32)
            place = slice(k * tile, (k + 1) * tile)
            residue = (
                (predicted[row * panel_tiles + col] - ratings[step, k].astype(F32)) * live
            ).astype(BF16)
            picked_items[place] = panel[col]
            picked_users[place] = user_table[row]
            for u in range(user_tiles):
                by_user[u * tile : (u + 1) * tile, place] = residue * hot(row, u)
            for p in range(panel_tiles):
                by_item[place, p * tile : (p + 1) * tile] = residue * hot(col, p)
        for q in range(user_tiles // 2):
            both = slice(2 * q * tile, 2 * (q + 1) * tile)
            user_sum[both] += jnp.dot(
                by_user[both], picked_items[...], preferred_element_type=F32
            )

            @pl.when(step == n_blk - 1)
            def _(q=q):
                pair_copy(q).start()

        item_send[step] = lax.dot_general(
            by_item[...],
            picked_users[...],
            (((0,), (0,)), ((), ())),
            preferred_element_type=F32,
        )

        @pl.when(step > 0)
        def _():
            item_copy(step).start()

        return carry

    lax.fori_loop(0, n_blk, visit, 0)

    def hop(t, carry):
        @pl.when(t < chunks)
        def _():
            c = t

            @pl.when(c % per_tile == 0)
            def _():
                pair_copy(c // per_tile).wait_recv()

            mine = pair_recv.at[pl.ds(c * CHUNK, CHUNK)]
            mine[...] += user_sum[own_rows(c, core)]

            @pl.when(has_near)
            def _():
                arrived(0, c).wait_recv()

            side_send[0, c] = mine[...] + side_recv[0, c]
            far_copy(c).start()

        @pl.when(t >= LAG)
        def _():
            c = t - LAG
            mine = pair_recv.at[pl.ds(c * CHUNK, CHUNK)]
            arrived(1, c).wait_recv()

            @pl.when(has_near)
            def _():
                side_send[1, c] = mine[...] + side_recv[1, c]
                near_copy(c).start()

            user_out[own_rows(c, core)] = (
                mine[...] + side_recv[0, c] + side_recv[1, c]
            ) * (1.0 / tile)
            share_copy(c).start()

        return carry

    lax.fori_loop(0, chunks + LAG, hop, 0)

    def settle(step, carry):
        item_copy(step).wait_recv()
        item_send[0] += item_recv[step]
        return carry

    lax.fori_loop(1, n_blk, settle, 0)
    item_out[...] = item_send[0] * (1.0 / tile)

    def drain_steps(step, carry):
        gather_copy(step).wait_send()
        item_copy(step).wait_send()
        return carry

    lax.fori_loop(1, n_blk, drain_steps, 0)

    def drain_pairs(q, carry):
        pair_copy(q).wait_send()
        return carry

    lax.fori_loop(0, user_tiles // 2, drain_pairs, 0)

    def drain_chunks(c, carry):
        far_copy(c).wait_send()

        @pl.when(has_near)
        def _():
            near_copy(c).wait_send()

        share_copy(c).wait_send()
        share_arrival(c).wait_recv()
        return carry

    lax.fori_loop(0, chunks, drain_chunks, 0)


def body(user_factors, item_factors, ratings, tile_user, tile_item, tile_count):
    n_blk = lax.axis_size("blk")
    n_strata = lax.axis_size("strata")
    user_rows, rank = user_factors.shape
    panel_rows = item_factors.shape[0]
    slots, tile = ratings.shape[-3], ratings.shape[-1]
    user_tiles, panel_tiles = user_rows // tile, panel_rows // tile
    chunks = user_rows // 2 // CHUNK
    dma = pltpu.SemaphoreType.DMA
    return pl.pallas_call(
        functools.partial(kernel, n_blk, n_strata),
        out_shape=(
            jax.ShapeDtypeStruct((user_rows, rank), F32),
            jax.ShapeDtypeStruct((panel_rows, rank), F32),
        ),
        in_specs=[pl.BlockSpec(memory_space=pl.ANY)] * 3
        + [pl.BlockSpec(memory_space=pltpu.SMEM)] * 3,
        out_specs=(
            pl.BlockSpec(memory_space=pltpu.VMEM),
            pl.BlockSpec(memory_space=pltpu.VMEM),
        ),
        scratch_shapes=[
            pltpu.VMEM((user_rows, rank), BF16),
            pltpu.VMEM((user_tiles, tile, rank), BF16),
            pltpu.VMEM((n_blk, panel_rows, rank), BF16),
            pltpu.VMEM((panel_tiles, tile, rank), BF16),
            pltpu.VMEM((n_blk, slots, tile, tile), BF16),
            pltpu.VMEM((user_tiles * panel_tiles, tile, tile), F32),
            pltpu.VMEM((slots * tile, rank), BF16),
            pltpu.VMEM((slots * tile, rank), BF16),
            pltpu.VMEM((user_rows, slots * tile), BF16),
            pltpu.VMEM((slots * tile, panel_rows), BF16),
            pltpu.VMEM((user_rows, rank), F32),
            pltpu.VMEM((n_blk, panel_rows, rank), F32),
            pltpu.VMEM((n_blk, panel_rows, rank), F32),
            pltpu.VMEM((user_rows // 2, rank), F32),
            pltpu.VMEM((2, chunks, CHUNK, rank), F32),
            pltpu.VMEM((2, chunks, CHUNK, rank), F32),
            dma((2,)),
            dma((n_blk,)),
            dma((n_blk,)),
            dma((n_blk,)),
            dma((n_blk,)),
            dma((n_blk,)),
            dma((user_tiles // 2,)),
            dma((user_tiles // 2,)),
            dma((2, chunks)),
            dma((2, chunks)),
            dma((chunks,)),
            dma((chunks,)),
        ],
        compiler_params=pltpu.CompilerParams(
            collective_id=0, has_side_effects=True, vmem_limit_bytes=48 << 20
        ),
    )(user_factors, item_factors, ratings, tile_user, tile_item, tile_count)


def solution(mesh):
    in_specs = (
        P("blk", None),
        P(("blk", "strata"), None),
        P("blk", None, "strata", None, None, None),
        P("blk", None, "strata", None),
        P("blk", None, "strata", None),
        P("blk", None, "strata"),
    )
    out_specs = (P("blk", None), P(("blk", "strata"), None))
    return jax.shard_map(body, mesh=mesh, in_specs=in_specs, out_specs=out_specs, check_vma=False)
```

time: 120 us -> 75.6 us (0.63)
  Pallas kernels: 0 us -> 68.4 us
  waiting for transfers between devices: 49.4 us -> 0 us
  matrix products: 20.7 us -> 0 us
  between operations: 15.9 us -> 0.65 us
  blocking collectives: 11.8 us -> 0 us
  local copies, waits for them, and re-layouts: 16.9 us -> 6.28 us
  other arithmetic: 4.39 us -> 0 us
    pallas_call x0 -> x1, Pallas kernels: none -> 68.4 us  [body(): pl.pallas_call(functools.partial(kernel, n_blk, n_strata), out_shape=(jax...]
    psum x1 -> x0, waiting for transfers between devices: 49.4 us -> none  [body(): user_grad = lax.psum(user_total, 'strata')]
    dot_general x20 -> x0, matrix products: 20.7 us -> none  [the longest x4 6.31 us: tile_terms(): jnp.einsum('kar,kbr->kab', picked_users, picked_items, preferred_element_...]
    all_gather x1 -> x0, blocking collectives: 11.8 us -> none  [body(): gathered = lax.all_gather(item_factors, 'blk', axis=0, tiled=True)]
    gather x8 -> x0, local copies, waits for them, and re-layouts: 8.62 us -> none  [the longest x4 5.5 us: tile_terms(): picked_items = jnp.take(panel_tiles, cols, axis=0)]
    convert_element_type x4 -> x0, other arithmetic: 2.57 us -> none  [tile_terms(): live = (jnp.arange(slots) < count).astype(jnp.float32)]
    add x1 -> x0, local copies, waits for them, and re-layouts: 1.29 us -> none  [body(): user_total = user_total + user_part]
    unnamed x39 -> x13, local copies, waits for them, and re-layouts: 6.27 us -> 6.28 us
  transfers between devices with their start and end apart: 2 -> 0, of which waited for: 1 -> 0; matrix products, arithmetic and copies ran while one was open for 6% -> 0% of each run, Pallas kernels for 0% -> 0%
where the time goes in v1:
time: 75.6 us; the launch traced here: 75.4 us
  Pallas kernels  68.4 us (90%)
  local copies, waits for them, and re-layouts  6.28 us (8%)
    pallas_call x1, Pallas kernels, body(): pl.pallas_call(functools.partial(kernel, n_blk, n_strata), out_shape=(jax...  68.4 us
    unnamed x13, local copies, waits for them, and re-layouts  6.28 us

profile of v1, /device:TPU:0, one launch (start us, length us, event | category | flops | bytes accessed | tf_op | source)
XLA Modules:
  0.0 75.4 jit_solution(17755080901591506861)
XLA Ops:
  0.6 0.0 copy-start.3
  0.6 0.7 copy.8.count_ref
  1.4 0.0 copy-done.3
  1.4 0.0 copy-start
  1.4 1.2 %copy-done = bf16[1,4,1,8,128,128]{5,4,3,2,1,0:T(8,128)(2,1)S(1)} copy-done((bf16[1,4,1,8,128,128]{5,4,3,2,1,0:T(8,128)(2,1)S(1)}, bf16[1,4,1,8,128,128]{5,4,3,2,1,0:T(8,128)(2,1)}, u32[]{:S(2)}) %copy-start) | copy-done | bytes 1048600
  2.6 0.0 copy-start.1
  2.6 1.0 %copy-done.1 = bf16[1024,256]{1,0:T(8,128)(2,1)S(1)} copy-done((bf16[1024,256]{1,0:T(8,128)(2,1)S(1)}, bf16[1024,256]{1,0:T(8,128)(2,1)}, u32[]{:S(2)}) %copy-start.1) | copy-done | bytes 524312
  3.7 0.0 copy-start.2
  3.7 0.9 %copy-done.2 = bf16[256,256]{1,0:T(8,128)(2,1)S(1)} copy-done((bf16[256,256]{1,0:T(8,128)(2,1)S(1)}, bf16[256,256]{1,0:T(8,128)(2,1)}, u32[]{:S(2)}) %copy-start.2) | copy-done | bytes 131096
  4.6 0.0 copy-start.4
  4.6 0.7 copy-done.4
  5.2 68.4 %shard_map.77 = (f32[1024,256]{1,0:T(8,128)S(1)}, f32[256,256]{1,0:T(8,128)S(1)}) custom-call(bf16[1024,256]{1,0:T(8,128)(2,1)S(1)} %copy-done.1, bf16[256,256]{1,0:T(8,128)(2,1)S(1)} %copy-done.2, bf16[1,4,1,8,128,128]{5,4,3,2,1,0:T(8,128)(2,1)S(1)} %copy-done, s32[1,4,1,8]{3,2,1,0:T(1,128)S(1)} %copy-done.3, s32[1,4,1,8]{3,2,1,0:T(1,128)S(1)} %copy-done.4, ...), custom_call_target="tpu_custom_call" | custom-call | tf_op jit(solution)/shard_map/pallas_call | solution.py:367
  73.7 1.0 %copy.11 = f32[1024,256]{1,0:T(8,128)} copy(f32[1024,256]{1,0:T(8,128)S(1)} %get-tuple-element.4) | data formatting | bytes 2097152
  74.7 0.7 copy.12
Async XLA Ops:
  0.6 0.8 %copy-start.3 = (s32[1,4,1,8]{3,2,1,0:T(1,128)S(1)}, s32[1,4,1,8]{3,2,1,0:T(1,128)}, u32[]{:S(2)}) copy-start(s32[1,4,1,8]{3,2,1,0:T(1,128)} %rows_ref.1) | copy-start | bytes 388
  1.4 1.2 %copy-start = (bf16[1,4,1,8,128,128]{5,4,3,2,1,0:T(8,128)(2,1)S(1)}, bf16[1,4,1,8,128,128]{5,4,3,2,1,0:T(8,128)(2,1)}, u32[]{:S(2)}) copy-start(bf16[1,4,1,8,128,128]{5,4,3,2,1,0:T(8,128)(2,1)} %ratings_hbm.1) | copy-start | bytes 3145732
  2.6 1.0 %copy-start.1 = (bf16[1024,256]{1,0:T(8,128)(2,1)S(1)}, bf16[1024,256]{1,0:T(8,128)(2,1)}, u32[]{:S(2)}) copy-start(bf16[1024,256]{1,0:T(8,128)(2,1)} %users_hbm.1) | copy-start | bytes 1572868
  3.7 0.9 %copy-start.2 = (bf16[256,256]{1,0:T(8,128)(2,1)S(1)}, bf16[256,256]{1,0:T(8,128)(2,1)}, u32[]{:S(2)}) copy-start(bf16[256,256]{1,0:T(8,128)(2,1)} %items_hbm.1) | copy-start | bytes 393220
  4.6 0.7 copy-start.4

commit v2 on v1

--- a/solution.py
+++ b/solution.py
@@ -11,7 +11,8 @@
 F32 = jnp.float32
 BF16 = jnp.bfloat16
 CHUNK = 64
-LAG = 2
+LAG = 3
+STEP_LAG = 5
 
 
 def flip(place, step, size):
@@ -81,6 +82,7 @@
     near = (chip - sign) * 2 + core
     depth = chip + upper * (chips - 1 - 2 * chip)
     has_near = depth > 0
+    lag = LAG + STEP_LAG * (half - 1 - depth)
     crossing = depth // (half - 1) if half > 1 else depth + 1
 
     load = pltpu.make_async_copy(users_hbm, users, load_sem.at[0])
@@ -300,9 +302,9 @@
             side_send[0, c] = mine[...] + side_recv[0, c]
             far_copy(c).start()
 
-        @pl.when(t >= LAG)
+        @pl.when(t >= lag)
         def _():
-            c = t - LAG
+            c = t - lag
             mine = pair_recv.at[pl.ds(c * CHUNK, CHUNK)]
             arrived(1, c).wait_recv()
 
@@ -318,7 +320,7 @@
 
         return carry
 
-    lax.fori_loop(0, chunks + LAG, hop, 0)
+    lax.fori_loop(0, chunks + lag, hop, 0)
 
     def settle(step, carry):
         item_copy(step).wait_recv()
@@ -370,7 +372,7 @@
             jax.ShapeDtypeStruct((user_rows, rank), F32),
             jax.ShapeDtypeStruct((panel_rows, rank), F32),
         ),
-        in_specs=[pl.BlockSpec(memory_space=pl.ANY)] * 3
+        in_specs=[pl.BlockSpec(memory_space=pltpu.HBM)] * 3
         + [pl.BlockSpec(memory_space=pltpu.SMEM)] * 3,
         out_specs=(
             pl.BlockSpec(memory_space=pltpu.VMEM),

time: 75.6 us -> 49.4 us (0.65)
  Pallas kernels: 68.4 us -> 42.2 us
    pallas_call x1, Pallas kernels: 68.4 us -> 42.2 us  [body(): pl.pallas_call(functools.partial(kernel, n_blk, n_strata), out_shape=(jax...]
where the time goes in v2:
time: 49.4 us; the launch traced here: 49.1 us
  Pallas kernels  42.2 us (85%)
  local copies, waits for them, and re-layouts  6.28 us (13%)
  between operations  0.65 us (1%)
    pallas_call x1, Pallas kernels, body(): pl.pallas_call(functools.partial(kernel, n_blk, n_strata), out_shape=(jax...  42.2 us
    unnamed x13, local copies, waits for them, and re-layouts  6.28 us

profile of v2, /device:TPU:0, one launch (start us, length us, event | category | flops | bytes accessed | tf_op | source)
XLA Modules:
  0.0 49.1 jit_solution(458851410878830958)
XLA Ops:
  0.6 0.0 copy-start.3
  0.6 0.7 %copy.8.count_ref = s32[1,4,1]{2,1,0:T(4,128)S(1)} copy(s32[1,4,1]{1,2,0:T(1,128)} %param.11) | data formatting | bytes 32 | tf_op args[5]
  1.4 0.0 copy-done.3
  1.4 0.0 copy-start
  1.4 1.2 %copy-done = bf16[1,4,1,8,128,128]{5,4,3,2,1,0:T(8,128)(2,1)S(1)} copy-done((bf16[1,4,1,8,128,128]{5,4,3,2,1,0:T(8,128)(2,1)S(1)}, bf16[1,4,1,8,128,128]{5,4,3,2,1,0:T(8,128)(2,1)}, u32[]{:S(2)}) %copy-start) | copy-done | bytes 1048600
  2.6 0.0 copy-start.1
  2.6 1.0 %copy-done.1 = bf16[1024,256]{1,0:T(8,128)(2,1)S(1)} copy-done((bf16[1024,256]{1,0:T(8,128)(2,1)S(1)}, bf16[1024,256]{1,0:T(8,128)(2,1)}, u32[]{:S(2)}) %copy-start.1) | copy-done | bytes 524312
  3.7 0.0 copy-start.2
  3.7 0.9 %copy-done.2 = bf16[256,256]{1,0:T(8,128)(2,1)S(1)} copy-done((bf16[256,256]{1,0:T(8,128)(2,1)S(1)}, bf16[256,256]{1,0:T(8,128)(2,1)}, u32[]{:S(2)}) %copy-start.2) | copy-done | bytes 131096
  4.6 0.0 copy-start.4
  4.6 0.7 %copy-done.4 = s32[1,4,1,8]{3,2,1,0:T(1,128)S(1)} copy-done((s32[1,4,1,8]{3,2,1,0:T(1,128)S(1)}, s32[1,4,1,8]{3,2,1,0:T(1,128)}, u32[]{:S(2)}) %copy-start.4) | copy-done | bytes 152
  5.2 42.2 %shard_map.77 = (f32[1024,256]{1,0:T(8,128)S(1)}, f32[256,256]{1,0:T(8,128)S(1)}) custom-call(bf16[1024,256]{1,0:T(8,128)(2,1)S(1)} %copy-done.1, bf16[256,256]{1,0:T(8,128)(2,1)S(1)} %copy-done.2, bf16[1,4,1,8,128,128]{5,4,3,2,1,0:T(8,128)(2,1)S(1)} %copy-done, s32[1,4,1,8]{3,2,1,0:T(1,128)S(1)} %copy-done.3, s32[1,4,1,8]{3,2,1,0:T(1,128)S(1)} %copy-done.4, ...), custom_call_target="tpu_custom_call" | custom-call | tf_op jit(solution)/shard_map/pallas_call | solution.py:369
  47.4 1.0 %copy.11 = f32[1024,256]{1,0:T(8,128)} copy(f32[1024,256]{1,0:T(8,128)S(1)} %get-tuple-element.4) | data formatting | bytes 2097152
  48.4 0.7 %copy.12 = f32[256,256]{1,0:T(8,128)} copy(f32[256,256]{1,0:T(8,128)S(1)} %get-tuple-element.5) | data formatting | bytes 524288
Async XLA Ops:
  0.6 0.8 %copy-start.3 = (s32[1,4,1,8]{3,2,1,0:T(1,128)S(1)}, s32[1,4,1,8]{3,2,1,0:T(1,128)}, u32[]{:S(2)}) copy-start(s32[1,4,1,8]{3,2,1,0:T(1,128)} %rows_ref.1) | copy-start | bytes 388
  1.4 1.2 %copy-start = (bf16[1,4,1,8,128,128]{5,4,3,2,1,0:T(8,128)(2,1)S(1)}, bf16[1,4,1,8,128,128]{5,4,3,2,1,0:T(8,128)(2,1)}, u32[]{:S(2)}) copy-start(bf16[1,4,1,8,128,128]{5,4,3,2,1,0:T(8,128)(2,1)} %ratings_hbm.1) | copy-start | bytes 3145732
  2.6 1.0 %copy-start.1 = (bf16[1024,256]{1,0:T(8,128)(2,1)S(1)}, bf16[1024,256]{1,0:T(8,128)(2,1)}, u32[]{:S(2)}) copy-start(bf16[1024,256]{1,0:T(8,128)(2,1)} %users_hbm.1) | copy-start | bytes 1572868
  3.7 0.9 %copy-start.2 = (bf16[256,256]{1,0:T(8,128)(2,1)S(1)}, bf16[256,256]{1,0:T(8,128)(2,1)}, u32[]{:S(2)}) copy-start(bf16[256,256]{1,0:T(8,128)(2,1)} %items_hbm.1) | copy-start | bytes 393220
  4.6 0.7 %copy-start.4 = (s32[1,4,1,8]{3,2,1,0:T(1,128)S(1)}, s32[1,4,1,8]{3,2,1,0:T(1,128)}, u32[]{:S(2)}) copy-start(s32[1,4,1,8]{3,2,1,0:T(1,128)} %cols_ref.1) | copy-start | bytes 388

commit v3 on v2

--- a/solution.py
+++ b/solution.py
@@ -11,8 +11,8 @@
 F32 = jnp.float32
 BF16 = jnp.bfloat16
 CHUNK = 64
-LAG = 3
-STEP_LAG = 5
+LAG = 2
+STEP_LAG = 6
 
 
 def flip(place, step, size):
@@ -37,14 +37,12 @@
     users,
     user_table,
     panels,
-    panel,
     ratings,
     predicted,
-    picked_items,
     picked_users,
-    by_user,
     by_item,
     user_sum,
+    parts,
     item_send,
     item_recv,
     pair_recv,
@@ -66,7 +64,7 @@
     tile = ratings.shape[-1]
     slots = ratings.shape[1]
     user_tiles = user_table.shape[0]
-    panel_tiles = panel.shape[0]
+    panel_tiles = panels.shape[1] // tile
     chunks = pair_recv.shape[0] // CHUNK
     per_tile = tile // CHUNK
     blk = lax.axis_index("blk")
@@ -211,7 +209,6 @@
         return carry
 
     lax.fori_loop(1, n_blk, start_gather, 0)
-    user_sum[...] = jnp.zeros_like(user_sum)
 
     @pl.when(depth == 0)
     def _():
@@ -234,7 +231,6 @@
             gather_copy(step).wait_recv()
 
         rating_copy(step).wait()
-        panel[...] = panels[step].reshape(panel.shape)
         for u in range(user_tiles):
             product = lax.dot_general(
                 users[u * tile : (u + 1) * tile],
@@ -252,22 +248,10 @@
             residue = (
                 (predicted[row * panel_tiles + col] - ratings[step, k].astype(F32)) * live
             ).astype(BF16)
-            picked_items[place] = panel[col]
             picked_users[place] = user_table[row]
-            for u in range(user_tiles):
-                by_user[u * tile : (u + 1) * tile, place] = residue * hot(row, u)
             for p in range(panel_tiles):
                 by_item[place, p * tile : (p + 1) * tile] = residue * hot(col, p)
-        for q in range(user_tiles // 2):
-            both = slice(2 * q * tile, 2 * (q + 1) * tile)
-            user_sum[both] += jnp.dot(
-                by_user[both], picked_items[...], preferred_element_type=F32
-            )
-
-            @pl.when(step == n_blk - 1)
-            def _(q=q):
-                pair_copy(q).start()
-
+        parts[step] = jnp.dot(by_item[...], panels[step], preferred_element_type=F32)
         item_send[step] = lax.dot_general(
             by_item[...],
             picked_users[...],
@@ -283,7 +267,29 @@
 
     lax.fori_loop(0, n_blk, visit, 0)
 
+    def gather_terms(q):
+        block = tile // 2
+        for start in (0, block):
+            sums = [jnp.zeros((block, user_sum.shape[-1]), F32)] * 2
+            for step in range(n_blk):
+                source = flip(blk, step, n_blk)
+                for k in range(slots):
+                    row = rows_ref[0, source, 0, k]
+                    term = parts[step, k * tile + start : k * tile + start + block]
+                    for one in range(2):
+                        same = (row == 2 * q + one).astype(F32)
+                        sums[one] = sums[one] + term * same
+            for one in range(2):
+                user_sum[pl.ds((2 * q + one) * tile + start, block)] = sums[one]
+        pair_copy(q).start()
+
+    gather_terms(0)
+
     def hop(t, carry):
+        @pl.when((t < chunks - per_tile) & (t % per_tile == 0))
+        def _():
+            gather_terms(t // per_tile + 1)
+
         @pl.when(t < chunks)
         def _():
             c = t
@@ -382,14 +388,12 @@
             pltpu.VMEM((user_rows, rank), BF16),
             pltpu.VMEM((user_tiles, tile, rank), BF16),
             pltpu.VMEM((n_blk, panel_rows, rank), BF16),
-            pltpu.VMEM((panel_tiles, tile, rank), BF16),
             pltpu.VMEM((n_blk, slots, tile, tile), BF16),
             pltpu.VMEM((user_tiles * panel_tiles, tile, tile), F32),
             pltpu.VMEM((slots * tile, rank), BF16),
-            pltpu.VMEM((slots * tile, rank), BF16),
-            pltpu.VMEM((user_rows, slots * tile), BF16),
             pltpu.VMEM((slots * tile, panel_rows), BF16),
             pltpu.VMEM((user_rows, rank), F32),
+            pltpu.VMEM((n_blk, slots * tile, rank), F32),
             pltpu.VMEM((n_blk, panel_rows, rank), F32),
             pltpu.VMEM((n_blk, panel_rows, rank), F32),
             pltpu.VMEM((user_rows // 2, rank), F32),
@@ -409,7 +413,7 @@
             dma((chunks,)),
         ],
         compiler_params=pltpu.CompilerParams(
-            collective_id=0, has_side_effects=True, vmem_limit_bytes=48 << 20
+            collective_id=0, has_side_effects=True, vmem_limit_bytes=60 << 20
         ),
     )(user_factors, item_factors, ratings, tile_user, tile_item, tile_count)
 

time: 49.4 us -> 44.8 us (0.907)
  Pallas kernels: 42.2 us -> 39.7 us
  local copies, waits for them, and re-layouts: 6.28 us -> 4.32 us
    pallas_call x1, Pallas kernels: 42.2 us -> 39.7 us  [body(): pl.pallas_call(functools.partial(kernel, n_blk, n_strata), out_shape=(jax...]
    unnamed x13 -> x5, local copies, waits for them, and re-layouts: 6.28 us -> 4.32 us
where the time goes in v3:
time: 44.8 us; the launch traced here: 44.6 us
  Pallas kernels  39.7 us (89%)
  local copies, waits for them, and re-layouts  4.32 us (10%)
  between operations  0.65 us (1%)
    pallas_call x1, Pallas kernels, body(): pl.pallas_call(functools.partial(kernel, n_blk, n_strata), out_shape=(jax...  39.7 us
    unnamed x5, local copies, waits for them, and re-layouts  4.32 us

profile of v3, /device:TPU:0, one launch (start us, length us, event | category | flops | bytes accessed | tf_op | source)
XLA Modules:
  0.0 44.6 jit_solution(13331298058430939191)
XLA Ops:
  0.6 1.3 %copy.8.count_ref = s32[1,4,1]{2,1,0:T(4,128)} copy(s32[1,4,1]{1,2,0:T(1,128)} %param.11) | data formatting | bytes 32 | tf_op args[5]
  1.9 39.7 %shard_map.77 = (f32[1024,256]{1,0:T(8,128)}, f32[256,256]{1,0:T(8,128)}) custom-call(bf16[1024,256]{1,0:T(8,128)(2,1)} %users_hbm.1, bf16[256,256]{1,0:T(8,128)(2,1)} %items_hbm.1, bf16[1,4,1,8,128,128]{5,4,3,2,1,0:T(8,128)(2,1)} %ratings_hbm.1, s32[1,4,1,8]{3,2,1,0:T(1,128)} %rows_ref.1, s32[1,4,1,8]{3,2,1,0:T(1,128)} %cols_ref.1, s32[1,4,1]{2,1,0:T(4,128)} %copy.8.count_ref), custom_call_target="tpu_custom_call" | custom-call | tf_op jit(solution)/shard_map/pallas_call | solution.py:375
  41.6 0.0 copy-start
  41.6 2.3 %copy.11 = f32[1024,256]{1,0:T(8,128)} copy(f32[1024,256]{1,0:T(8,128)} %get-tuple-element.4) | data formatting | bytes 2097152
  43.9 0.0 copy-done
  43.9 0.7 %copy.12 = f32[256,256]{1,0:T(8,128)} copy(f32[256,256]{1,0:T(8,128)S(1)} %copy-done) | data formatting | bytes 524288
Async XLA Ops:
  41.6 2.3 %copy-start = (f32[256,256]{1,0:T(8,128)S(1)}, f32[256,256]{1,0:T(8,128)}, u32[]{:S(2)}) copy-start(f32[256,256]{1,0:T(8,128)} %get-tuple-element.5) | copy-start | bytes 786436

commit v4 on v3

--- a/solution.py
+++ b/solution.py
@@ -243,7 +243,7 @@
         for k in range(slots):
             row = rows_ref[0, source, 0, k]
             col = cols_ref[0, source, 0, k]
-            live = (k < count_ref[0, source, 0]).astype(F32)
+            live = (k < count_ref[0, 0, source]).astype(F32)
             place = slice(k * tile, (k + 1) * tile)
             residue = (
                 (predicted[row * panel_tiles + col] - ratings[step, k].astype(F32)) * live
@@ -413,9 +413,13 @@
             dma((chunks,)),
         ],
         compiler_params=pltpu.CompilerParams(
-            collective_id=0, has_side_effects=True, vmem_limit_bytes=60 << 20
+            collective_id=0, has_side_effects=True, vmem_limit_bytes=48 << 20
         ),
-    )(user_factors, item_factors, ratings, tile_user, tile_item, tile_count)
+    )(
+        pltpu.with_memory_space_constraint(user_factors, pltpu.HBM),
+        pltpu.with_memory_space_constraint(item_factors, pltpu.HBM),
+        pltpu.with_memory_space_constraint(ratings, pltpu.HBM),
+        tile_user, tile_item, jnp.swapaxes(tile_count, 1, 2))
 
 
 def solution(mesh):

time: 44.8 us -> 43 us (0.960)
  Pallas kernels: 39.7 us -> 38.5 us
  local copies, waits for them, and re-layouts: 4.32 us -> 3.69 us
    pallas_call x1, Pallas kernels: 39.7 us -> 38.5 us  [body(): pl.pallas_call(functools.partial(kernel, n_blk, n_strata), out_shape=(jax...]
    unnamed x5 -> x8, local copies, waits for them, and re-layouts: 4.32 us -> 3.69 us
where the time goes in v4:
time: 43 us; the launch traced here: 42.8 us
  Pallas kernels  38.5 us (90%)
  local copies, waits for them, and re-layouts  3.69 us (9%)
  between operations  0.65 us (2%)
    pallas_call x1, Pallas kernels, body(): pl.pallas_call(functools.partial(kernel, n_blk, n_strata), out_shape=(jax...  38.5 us
    unnamed x8, local copies, waits for them, and re-layouts  3.69 us

profile of v4, /device:TPU:0, one launch (start us, length us, event | category | flops | bytes accessed | tf_op | source)
XLA Modules:
  0.0 42.8 jit_solution(6539868458708882892)
XLA Ops:
  0.6 0.0 copy-start.2
  0.6 0.6 %copy-done.2 = s32[1,4,1]{1,2,0:T(1,128)S(1)} copy-done((s32[1,4,1]{1,2,0:T(1,128)S(1)}, s32[1,4,1]{1,2,0:T(1,128)}, u32[]{:S(2)}) %copy-start.2) | copy-done | bytes 40
  1.3 0.0 copy-start
  1.3 0.7 %copy-done = s32[1,4,1,8]{3,2,1,0:T(1,128)S(1)} copy-done((s32[1,4,1,8]{3,2,1,0:T(1,128)S(1)}, s32[1,4,1,8]{3,2,1,0:T(1,128)}, u32[]{:S(2)}) %copy-start) | copy-done | bytes 152
  2.0 0.0 copy-start.1
  2.0 0.7 %copy-done.1 = s32[1,4,1,8]{3,2,1,0:T(1,128)S(1)} copy-done((s32[1,4,1,8]{3,2,1,0:T(1,128)S(1)}, s32[1,4,1,8]{3,2,1,0:T(1,128)}, u32[]{:S(2)}) %copy-start.1) | copy-done | bytes 152
  2.7 38.5 %shard_map.77 = (f32[1024,256]{1,0:T(8,128)S(1)}, f32[256,256]{1,0:T(8,128)S(1)}) custom-call(bf16[1024,256]{1,0:T(8,128)(2,1)} %users_hbm.1, bf16[256,256]{1,0:T(8,128)(2,1)} %items_hbm.1, bf16[1,4,1,8,128,128]{5,4,3,2,1,0:T(8,128)(2,1)} %ratings_hbm.1, s32[1,4,1,8]{3,2,1,0:T(1,128)S(1)} %copy-done, s32[1,4,1,8]{3,2,1,0:T(1,128)S(1)} %copy-done.1, ...), custom_call_target="tpu_custom_call" | custom-call | tf_op jit(solution)/shard_map/pallas_call | solution.py:375
  41.1 1.0 %copy.10 = f32[1024,256]{1,0:T(8,128)} copy(f32[1024,256]{1,0:T(8,128)S(1)} %get-tuple-element.4) | data formatting | bytes 2097152
  42.1 0.7 %copy.11 = f32[256,256]{1,0:T(8,128)} copy(f32[256,256]{1,0:T(8,128)S(1)} %get-tuple-element.5) | data formatting | bytes 524288
Async XLA Ops:
  0.6 0.7 %copy-start.2 = (s32[1,4,1]{1,2,0:T(1,128)S(1)}, s32[1,4,1]{1,2,0:T(1,128)}, u32[]{:S(2)}) copy-start(s32[1,4,1]{1,2,0:T(1,128)} %param.11) | copy-start | bytes 52
  1.3 0.7 %copy-start = (s32[1,4,1,8]{3,2,1,0:T(1,128)S(1)}, s32[1,4,1,8]{3,2,1,0:T(1,128)}, u32[]{:S(2)}) copy-start(s32[1,4,1,8]{3,2,1,0:T(1,128)} %rows_ref.1) | copy-start | bytes 388
  2.0 0.7 %copy-start.1 = (s32[1,4,1,8]{3,2,1,0:T(1,128)S(1)}, s32[1,4,1,8]{3,2,1,0:T(1,128)}, u32[]{:S(2)}) copy-start(s32[1,4,1,8]{3,2,1,0:T(1,128)} %cols_ref.1) | copy-start | bytes 388
